TPU v7x, 256 devices: a whole 4x4x8 slice. The times are simulated.
256 devices in a mesh: gz: 32 (over y, z_lo, core), gx: 8 (over x, z_hi).
Axes of the slice: x: 4, y: 4, z: 8 (z_hi: 2, z_lo: 4; z = z_hi * 4 + z_lo), core: 2. Of those that a mesh axis runs over, the one named last changes fastest.
Arguments:
- ending_rightward_adjoint: float32 [2, 2048, 2048], P(None, 'gz', 'gx'), may hold values from -6 to 6
- ending_leftward_adjoint: float32 [2, 2048, 2048], P(None, 'gz', 'gx'), may hold values from -6 to 6
- ending_population_adjoint: float32 [2048, 2048], P('gz', 'gx'), may hold values from -6 to 6
- ending_holeburn_adjoint: float32 [2048, 2048], P('gz', 'gx'), may hold values from -6 to 6
- history_rightward: bfloat16 [4, 2, 2048, 2048], P(None, None, 'gz', 'gx'), may hold values from -4 to 4
- history_leftward: bfloat16 [4, 2, 2048, 2048], P(None, None, 'gz', 'gx'), may hold values from -4 to 4
- history_population: bfloat16 [4, 2048, 2048], P(None, 'gz', 'gx'), may hold values from 0.5 to 2
- history_holeburn: bfloat16 [4, 2048, 2048], P(None, 'gz', 'gx'), may hold values from -4 to 4
- segment_passive_attenuation: bfloat16 [2048, 2048], P('gz', 'gx'), may hold values from 0.049804688 to 0.59765625
Outputs:
- forward_adjoint: float32 [2, 2048, 2048], P(None, 'gz', 'gx')
- backward_adjoint: float32 [2, 2048, 2048], P(None, 'gz', 'gx')
- carrier_adjoint: float32 [2048, 2048], P('gz', 'gx')
- grating_adjoint: float32 [2048, 2048], P('gz', 'gx')
- current_gradient: float32 [2048], P('gx')
All inputs are finite; a program needn't handle non-finite values.
Results may differ from a plain program's by a relative error of at most 0.0004.
Values may be sent and summed in bfloat16 or wider, within the bound.
A program may use at most 64 MiB of HBM per device.

v0:
```python
import functools
import math

import jax
import jax.numpy as jnp
import numpy as np
from jax import lax
from jax.experimental import pallas as pl
from jax.experimental.pallas import tpu as pltpu
from jax.sharding import PartitionSpec as P

DIFF = 512
FRONT_FACET = 0.3
REAR_FACET = 0.9
GAIN_SLOPE_RATE = 0.3
ALPHA_LINEWIDTH = 2.0
COUPLING = 0.5
CLOCK_DELTA = 0.3
DENSITY_LIFETIME = 2.0
GRATING_LIFE = 0.75
TRANSVERSE_DIFFUS = 0.2

MESH = pl.DeviceIdType.MESH
F32 = jnp.float32
BF16 = jnp.bfloat16

NGX = 8
NGZ = 32
ROWS = 64
COLS = 256
OWN = 8
LANES = 128
RADIX = 16
WIDTH = 2048
POWER = 16.0
SPAN = 210.0
TINY = 1e-30


def tables():
    ka = np.arange(RADIX, dtype=np.float64)
    bb = np.arange(LANES, dtype=np.float64)
    twist = 2.0 * np.pi * ka[:, None] * bb[None, :] / WIDTH
    wavenum = np.arange(RADIX)[:, None] + RADIX * np.arange(LANES)[None, :]
    signed = np.where(wavenum < WIDTH // 2, wavenum, wavenum - WIDTH).astype(np.float64)
    phase = signed * signed * (DIFF / (WIDTH / 2) ** 2)
    small = np.stack(
        [np.cos(twist), np.sin(twist), np.cos(phase) / WIDTH, np.sin(phase) / WIDTH]
    ).astype(np.float32)
    angle = 2.0 * np.pi * ((bb[:, None] * bb[None, :]) % LANES) / LANES
    c, s = np.cos(angle), np.sin(angle)
    forward = np.block([[c, -s], [s, c]])
    inverse = np.block([[c, s], [-s, c]])
    mats = []
    for m in (forward, inverse):
        high = m.astype(np.float32).astype(jnp.bfloat16)
        low = (m - high.astype(np.float64)).astype(np.float32).astype(jnp.bfloat16)
        mats += [high, low]
    return np.stack(mats), small


def encode(v, inverse_scale):
    t = jnp.log2(1.0 + jnp.abs(v) * inverse_scale) * POWER
    return jnp.exp2(jnp.where(v < 0.0, -t, t))


def decode(y, scale):
    t = jnp.log2(y.astype(F32)) * (1.0 / POWER)
    u = (jnp.exp2(jnp.abs(t)) - 1.0) * scale
    return jnp.where(t < 0.0, -u, u)


def largest(block):
    return jnp.max(jnp.max(block, axis=0, keepdims=True), axis=1, keepdims=True)


def dft(values, sign):
    n = len(values)
    if n == 1:
        return values
    even = dft(values[0::2], sign)
    odd = dft(values[1::2], sign)
    low, high = [], []
    for k in range(n // 2):
        angle = 2.0 * math.pi * k / n
        c, s = math.cos(angle), sign * math.sin(angle)
        re, im = odd[k]
        if k == 0:
            tr, ti = re, im
        elif 4 * k == n:
            tr, ti = (-im, re) if s > 0 else (im, -re)
        elif 8 * k == n:
            h = c
            tr, ti = ((re - im) * h, (re + im) * h) if s > 0 else ((re + im) * h, (im - re) * h)
        elif 8 * k == 3 * n:
            h = -c
            tr, ti = ((-re - im) * h, (re - im) * h) if s > 0 else ((im - re) * h, (-re - im) * h)
        else:
            tr, ti = re * c - im * s, re * s + im * c
        er, ei = even[k]
        low.append((er + tr, ei + ti))
        high.append((er - tr, ei - ti))
    return low + high


def split(x):
    high = x.astype(BF16)
    return high, (x - high.astype(F32)).astype(BF16)


def product(xh, xl, w, which):
    high, low = w[2 * which], w[2 * which + 1]
    a = jnp.dot(xh[...], high, preferred_element_type=F32)
    a += jnp.dot(xl[...], high, preferred_element_type=F32)
    return a + jnp.dot(xh[...], low, preferred_element_type=F32)


def diffract(uv, out, w, tb, xh, xl):
    for field in range(2):
        points = [(uv[2 * field, a], uv[2 * field + 1, a]) for a in range(RADIX)]
        for k, (re, im) in enumerate(dft(points, -1.0)):
            c, s = tb[0, k : k + 1, :], tb[1, k : k + 1, :]
            row = pl.ds(16 * k + 8 * field, 8)
            h, l = split(re * c + im * s)
            xh[row, 0:LANES], xl[row, 0:LANES] = h, l
            h, l = split(im * c - re * s)
            xh[row, LANES:], xl[row, LANES:] = h, l
    spectrum = product(xh, xl, w, 0)
    for k in range(RADIX):
        row = slice(16 * k, 16 * k + 16)
        c, s = tb[2, k : k + 1, :], tb[3, k : k + 1, :]
        re, im = spectrum[row, :LANES], spectrum[row, LANES:]
        h, l = split(re * c - im * s)
        xh[row, 0:LANES], xl[row, 0:LANES] = h, l
        h, l = split(re * s + im * c)
        xh[row, LANES:], xl[row, LANES:] = h, l
    back = product(xh, xl, w, 1)
    for field in range(2):
        points = []
        for k in range(RADIX):
            row = slice(16 * k + 8 * field, 16 * k + 8 * field + 8)
            c, s = tb[0, k : k + 1, :], tb[1, k : k + 1, :]
            re, im = back[row, :LANES], back[row, LANES:]
            points.append((re * c - im * s, im * c + re * s))
        for a, (re, im) in enumerate(dft(points, 1.0)):
            out[2 * field, a] = re
            out[2 * field + 1, a] = im


def revised(v, wave, level, mirror, loss, c, m, lap):
    vfr, vfi, vbr, vbi = v
    fr, fi, br, bi = wave
    e = level - 1.0
    hr = 1.0 + 0.5 * (GAIN_SLOPE_RATE * e - loss)
    hi = 0.5 * GAIN_SLOPE_RATE * ALPHA_LINEWIDTH * e
    j = COUPLING * mirror
    pd = 2.0 * CLOCK_DELTA * GAIN_SLOPE_RATE * e * c
    hd = 2.0 * CLOCK_DELTA * m
    pr = hr * vfr - hi * vfi + j * vbi - pd * fr + hd * br
    pi = hr * vfi + hi * vfr - j * vbr - pd * fi + hd * bi
    qr = hr * vbr - hi * vbi + j * vfi - pd * br + hd * fr
    qi = hr * vbi + hi * vbr - j * vfr - pd * bi + hd * fi
    light = fr * fr + fi * fi + br * br + bi * bi
    share = (
        vfr * (fr + ALPHA_LINEWIDTH * fi)
        + vfi * (fi - ALPHA_LINEWIDTH * fr)
        + vbr * (br + ALPHA_LINEWIDTH * bi)
        + vbi * (bi - ALPHA_LINEWIDTH * br)
    )
    cn = (
        c * (1.0 - CLOCK_DELTA / DENSITY_LIFETIME - CLOCK_DELTA * GAIN_SLOPE_RATE * light)
        + TRANSVERSE_DIFFUS * lap
        + 0.5 * GAIN_SLOPE_RATE * share
    )
    mn = m * (1.0 - CLOCK_DELTA / GRATING_LIFE) + COUPLING * (
        vfi * br - vfr * bi + vbi * fr - vbr * fi
    )
    return pr, pi, qr, qi, cn, mn


def place_of(g, b):
    x, zh, core = lax.div(b, 2), lax.rem(b, 2), lax.rem(g, 2)
    pos = x + zh * (7 - 2 * x)
    return pos + core * (7 - 2 * pos)


def owner_of(g, j):
    core = lax.rem(g, 2)
    pos = j + core * (7 - 2 * j)
    far = lax.div(pos, 4)
    return 2 * pos * (1 - far) + (2 * (7 - pos) + 1) * far


def rows_at(j):
    return pl.ds(pl.multiple_of(j * OWN, OWN), OWN)


def iota(axis):
    return lax.broadcasted_iota(jnp.int32, (OWN, LANES), axis)


def exchange_kernel(
    p_h, q_h, c_h, m_h, f_h, b_h, n_h, g_h, l_h, w_h, t_h,
    oc, oe, os,
    pq, w, tb, ch, co, ax, rc, ra, rh, rl, st, uv, vv, xh, xl,
    hs, hr, sacc, sb, sr, s2b, s2, s3b, s3, vo, eo,
    ls, ss, rs, cs, cr, hss, hrs, ys, yr, zs, zr,
):
    g, b = lax.axis_index("gz"), lax.axis_index("gx")
    me = place_of(g, b)
    y, r = lax.div(g, 8), lax.rem(g, 8)
    started = []

    loads = [
        (p_h, pq.at[0:2]),
        (q_h, pq.at[2:4]),
        (c_h, pq.at[4]),
        (m_h, pq.at[5]),
        (w_h, w),
        (t_h, tb),
    ]
    loads = [pltpu.make_async_copy(a, d, ls.at[i]) for i, (a, d) in enumerate(loads)]
    for load in loads:
        load.start()

    g_up, g_down = lax.rem(g + 1, NGZ), lax.rem(g + NGZ - 1, NGZ)
    chain = g * NGX + me
    after = lax.rem(chain + 1, NGZ * NGX)
    before = lax.rem(chain + NGZ * NGX - 1, NGZ * NGX)

    def row_device(q):
        qg = lax.div(q, NGX)
        return qg, owner_of(qg, lax.rem(q, NGX))

    dev_after, dev_before = row_device(after), row_device(before)
    y_peers = [(lax.rem(y + k, 4) * 8 + r, b) for k in range(1, 4)]
    z_peers = [(y * 8 + lax.rem(r + k, 8), b) for k in range(1, 8)]
    x_peers = [(g, lax.rem(b + k, NGX)) for k in range(1, NGX)]
    greet = x_peers + y_peers + z_peers + [(g_up, b), (g_down, b), dev_after, dev_before]
    barrier = pltpu.get_barrier_semaphore()
    for peer in greet:
        pl.semaphore_signal(barrier, inc=1, device_id=peer, device_id_type=MESH)

    for load in loads[:4]:
        load.wait()
    top_c = largest(jnp.max(jnp.abs(pq[4]).reshape(8, 8, COLS), axis=0))
    top_m = largest(jnp.max(jnp.abs(pq[5]).reshape(8, 8, COLS), axis=0))
    top_u = jnp.max(jnp.abs(pq[0:4]).reshape(32, 8, COLS), axis=0)
    sc_c = jnp.maximum(top_c, TINY) * (1.0 / SPAN)
    sc_m = jnp.maximum(top_m, TINY) * (1.0 / SPAN)
    for i, sc in ((4, sc_c), (5, sc_m)):
        inv = 1.0 / sc
        for t in range(8):
            rows = slice(8 * t, 8 * t + 8)
            co[i, rows] = encode(pq[i, rows], inv).astype(BF16)

    pl.semaphore_wait(barrier, len(greet))

    def remote(src, dst, send, recv, device):
        copy = pltpu.make_async_remote_copy(
            src_ref=src, dst_ref=dst, send_sem=send, recv_sem=recv,
            device_id=device, device_id_type=MESH,
        )
        copy.start()
        started.append(copy)
        return copy

    edge = [
        remote(p_h.at[:, 0:8, :], ch.at[0], cs.at[0], cr.at[0], (g_down, b)),
        remote(q_h.at[:, 56:64, :], ch.at[1], cs.at[1], cr.at[1], (g_up, b)),
    ]

    def spread(ident, src_of, dst):
        got = []
        for k in range(1, NGX):
            peer = lax.rem(b + k, NGX)
            src = src_of(peer, place_of(g, peer))
            got.append(remote(src, dst, ss.at[ident, k], rs.at[ident, k], (g, peer)))
        own = pltpu.make_async_copy(src_of(b, me), dst, rs.at[ident, 0])
        own.start()
        return got, own

    def arrive(group):
        for copies, own in group:
            for copy in copies:
                copy.wait_recv()
            own.wait()

    def history(step):
        base = 3 + 4 * (3 - step) + (1 if step < 3 else 0)
        slot = rh.at[3 - step]
        return [
            spread(base, lambda _, j: f_h.at[step, :, rows_at(j), :], slot.at[0:2, b]),
            spread(base + 1, lambda _, j: b_h.at[step, :, rows_at(j), :], slot.at[2:4, b]),
            spread(base + 2, lambda _, j: n_h.at[step, rows_at(j), :], slot.at[4, b]),
            spread(base + 3, lambda _, j: g_h.at[step, rows_at(j), :], slot.at[5, b]),
        ]

    got_hist = {3: history(3)}
    got_loss = [spread(7, lambda _, j: l_h.at[rows_at(j), :], rl.at[b])]
    got_cm = [spread(0, lambda _, j: co.at[4:6, rows_at(j), :], rc.at[4:6, b])]

    for copy in edge:
        copy.wait_recv()
    halo = jnp.maximum(jnp.max(jnp.abs(ch[0]), axis=0), jnp.max(jnp.abs(ch[1]), axis=0))
    first_block, last_block = g == 0, g == NGZ - 1
    use_halo_top = jnp.where(first_block & last_block, 0.0, 1.0)
    top_u = largest(jnp.maximum(top_u, halo * use_halo_top))
    sc_u = jnp.maximum(top_u, TINY) * (1.0 / SPAN)
    inv = 1.0 / sc_u
    wide_row = lax.broadcasted_iota(jnp.int32, (OWN, COLS), 0)
    for part in range(2):
        for t in range(8):
            rows = slice(8 * t, 8 * t + 8)
            block = pltpu.roll(pq[part, rows], 7, 0)
            if t < 7:
                edge_row = pq[part, 8 * t + 8 : 8 * t + 9]
            else:
                edge_row = jnp.where(
                    last_block, FRONT_FACET * pq[2 + part, 63:64], ch[0, part, 0:1]
                )
            block = jnp.where(wide_row == 7, edge_row, block)
            co[part, rows] = encode(block, inv).astype(BF16)
            block = pltpu.roll(pq[2 + part, rows], 1, 0)
            if t > 0:
                edge_row = pq[2 + part, 8 * t - 1 : 8 * t]
            else:
                edge_row = jnp.where(first_block, REAR_FACET * pq[part, 0:1], ch[1, part, 7:8])
            block = jnp.where(wide_row == 0, edge_row, block)
            co[2 + part, rows] = encode(block, inv).astype(BF16)
    row, lane = iota(0), iota(1)
    ax[...] = jnp.where(row == 0, sc_u, jnp.where(row == 1, sc_c, sc_m))
    got_ax = [spread(2, lambda _, j: ax, ra.at[b])]
    got_uv = [spread(1, lambda _, j: co.at[0:4, rows_at(j), :], rc.at[0:4, b])]
    got_hist[2] = history(2)

    for load in loads[4:]:
        load.wait()
    arrive(got_ax)
    arrive(got_uv)
    for a in range(RADIX):
        src, half = a // 2, pl.ds(LANES * (a % 2), LANES)
        scale = ra[src, 0:1, :]
        for i in range(4):
            uv[i, a] = decode(rc[i, src, :, half], scale)
    got_hist[1] = history(1)
    diffract(uv, vv, w, tb, xh, xl)

    arrive(got_cm)
    arrive(got_loss)
    for a in range(RADIX):
        src, half = a // 2, pl.ds(LANES * (a % 2), LANES)
        for i in (4, 5):
            st[i, a] = decode(rc[i, src, :, half], ra[src, i - 3 : i - 2, :])
    weight = 1.0 + (2.0 / (ROWS * NGZ - 1)) * (row + chain * OWN).astype(F32)
    for a in range(RADIX):
        sacc[a] = weight * st[4, a]

    first_rows, last_rows = chain == 0, chain == NGZ * NGX - 1

    def lateral(a):
        c = st[4, a]
        left, right = pltpu.roll(c, 1, 1), pltpu.roll(c, LANES - 1, 1)
        left_in = pltpu.roll(st[4, a - 1], 1, 1) if a > 0 else jnp.zeros_like(c)
        right_in = (
            pltpu.roll(st[4, a + 1], LANES - 1, 1) if a < RADIX - 1 else jnp.zeros_like(c)
        )
        left = jnp.where(lane == 0, left_in, left)
        right = jnp.where(lane == LANES - 1, right_in, right)
        return c, left, right

    halos = None
    for step in (3, 2, 1):
        slot = 3 - step
        arrive(got_hist[step])
        laps = []
        for a in range(RADIX):
            c, left, right = lateral(a)
            uv[0, a] = right - 2.0 * c + left
        for a in range(RADIX):
            src, half = a // 2, pl.ds(LANES * (a % 2), LANES)
            past = [rh[slot, i, src, :, half].astype(F32) for i in range(6)]
            new = revised(
                [vv[i, a] for i in range(4)], past[:4], past[4], past[5],
                rl[src, :, half].astype(F32), st[4, a], st[5, a], uv[0, a],
            )
            for i in range(6):
                st[i, a] = new[i]
            sacc[a] += weight * new[4]
            for i in range(2):
                hs[slot, 0, i, :, pl.ds(LANES * a, LANES)] = new[i][0:1]
                hs[slot, 1, i, :, pl.ds(LANES * a, LANES)] = new[2 + i][7:8]
        halos = [
            remote(hs.at[slot, 0], hr.at[slot, 0], hss.at[slot, 0], hrs.at[slot, 0], dev_before),
            remote(hs.at[slot, 1], hr.at[slot, 1], hss.at[slot, 1], hrs.at[slot, 1], dev_after),
        ]
        if step == 1:
            for a in range(RADIX):
                half = pl.ds(LANES * (a % 2), LANES)
                sb[a // 2, :, half] = jnp.sum(sacc[a], axis=0, keepdims=True)
            got_s = [spread(19, lambda peer, j: sb.at[peer], sr.at[b])]
            scales = []
            for i in (4, 5):
                top = jnp.abs(st[i, 0])
                for a in range(1, RADIX):
                    top = jnp.maximum(top, jnp.abs(st[i, a]))
                sc = jnp.maximum(largest(top), TINY) * (1.0 / SPAN)
                scales.append(sc)
                inv = 1.0 / sc
                for a in range(RADIX):
                    half = pl.ds(LANES * (a % 2), LANES)
                    vo[i, a // 2, :, half] = encode(st[i, a], inv).astype(BF16)
            got_out = [spread(16, lambda peer, j: vo.at[4:6, peer], oc.at[4:6, me])]
        for copy in halos:
            copy.wait_recv()
        energy = [jnp.zeros((OWN, LANES), F32), jnp.zeros((OWN, LANES), F32)]
        for a in range(RADIX):
            cols = pl.ds(LANES * a, LANES)
            for i in range(2):
                edge_row = jnp.where(
                    last_rows, FRONT_FACET * st[2 + i, a, 7:8], hr[slot, 0, i, :, cols]
                )
                u = jnp.where(row == 7, edge_row, pltpu.roll(st[i, a], 7, 0))
                edge_row = jnp.where(
                    first_rows, REAR_FACET * st[i, a, 0:1], hr[slot, 1, i, :, cols]
                )
                q = jnp.where(row == 0, edge_row, pltpu.roll(st[2 + i, a], 1, 0))
                uv[i, a] = u
                uv[2 + i, a] = q
                if step == 1:
                    energy = [energy[0] + u * u, energy[1] + q * q]
        if step == 1:
            norms = [jnp.sum(e, axis=1, keepdims=True) for e in energy]
            norm = jnp.sqrt(jnp.max(jnp.maximum(norms[0], norms[1]), axis=0, keepdims=True))
            sc_v = jnp.maximum(norm, TINY) * (1.0 / SPAN)
            marks = jnp.where(row == 0, sc_v, jnp.where(row == 1, scales[0], scales[1]))
            for block in range(NGX):
                _, left, _ = lateral(2 * block)
                _, _, right = lateral(2 * block + 1)
                tile = jnp.where(lane == 0, left, marks)
                eo[block] = jnp.where(lane == LANES - 1, right, tile)
            got_out.append(spread(17, lambda peer, j: eo.at[peer], oe.at[me]))
            arrive(got_s)
            total = sr[0]
            for k in range(1, NGX):
                total = total + sr[k]
            s2b[...] = total
            s2[0] = total
            got_y = [
                remote(s2b, s2.at[k], ys.at[k], yr.at[k], peer)
                for k, peer in enumerate(y_peers, 1)
            ]
        diffract(uv, vv, w, tb, xh, xl)

    for copy in got_y:
        copy.wait_recv()
    total = (s2[0] + s2[1]) + (s2[2] + s2[3])
    s3b[...] = total
    s3[0] = total
    got_z = [
        remote(s3b, s3.at[k], zs.at[k], zr.at[k], peer) for k, peer in enumerate(z_peers, 1)
    ]
    inv = 1.0 / sc_v
    for a in range(RADIX):
        half = pl.ds(LANES * (a % 2), LANES)
        for i in range(4):
            vo[i, a // 2, :, half] = encode(vv[i, a], inv).astype(BF16)
    got_out.append(spread(18, lambda peer, j: vo.at[0:4, peer], oc.at[0:4, me]))
    for copy in got_z:
        copy.wait_recv()
    total = s3[0]
    for k in range(1, NGX):
        total = total + s3[k]
    os[...] = total * (CLOCK_DELTA / math.sqrt(ROWS * NGZ))
    arrive(got_out)
    for copy in started:
        copy.wait_send()


def final_kernel(oc, oe, os, f, bw, n, g, l, po, qo, co, mo, so, edge):
    so[...] = os[...]
    lane = lax.broadcasted_iota(jnp.int32, (OWN, COLS), 1)
    for t in range(oc.shape[1]):
        rows = pl.ds(OWN * t, OWN)
        marks = oe[t]
        scale = [marks[i : i + 1, 64:65] for i in range(3)]
        v = [decode(oc[i, t], scale[0]) for i in range(4)]
        c = decode(oc[4, t], scale[1])
        m = decode(oc[5, t], scale[2])
        left = jnp.where(lane == 0, marks[:, 0:1], pltpu.roll(c, 1, 1))
        right = jnp.where(lane == COLS - 1, marks[:, 127:128], pltpu.roll(c, COLS - 1, 1))
        wave = [x[0, i, rows].astype(F32) for x in (f, bw) for i in range(2)]
        new = revised(
            v, wave, n[0, rows].astype(F32), g[0, rows].astype(F32), l[rows].astype(F32),
            c, m, right - 2.0 * c + left,
        )
        po[0, rows], po[1, rows] = new[0], new[1]
        qo[0, rows], qo[1, rows] = new[2], new[3]
        co[rows] = new[4]
        mo[rows] = new[5]


def per_device(p, q, c, m, f, bw, n, g, l):
    mats, small = tables()
    any_space = pl.BlockSpec(memory_space=pl.ANY)
    dma = pltpu.SemaphoreType.DMA
    codes, edges, sums = pl.pallas_call(
        exchange_kernel,
        out_shape=(
            jax.ShapeDtypeStruct((6, NGX, OWN, COLS), BF16),
            jax.ShapeDtypeStruct((NGX, OWN, LANES), F32),
            jax.ShapeDtypeStruct((1, COLS), F32),
        ),
        in_specs=[any_space] * 11,
        out_specs=(any_space, any_space, pl.BlockSpec(memory_space=pltpu.VMEM)),
        scratch_shapes=[
            pltpu.VMEM((6, ROWS, COLS), F32),
            pltpu.VMEM((4, COLS, COLS), BF16),
            pltpu.VMEM((4, RADIX, LANES), F32),
            pltpu.VMEM((2, 2, OWN, COLS), F32),
            pltpu.VMEM((6, ROWS, COLS), BF16),
            pltpu.VMEM((OWN, LANES), F32),
            pltpu.VMEM((6, NGX, OWN, COLS), BF16),
            pltpu.VMEM((NGX, OWN, LANES), F32),
            pltpu.VMEM((3, 6, NGX, OWN, COLS), BF16),
            pltpu.VMEM((NGX, OWN, COLS), BF16),
            pltpu.VMEM((6, RADIX, OWN, LANES), F32),
            pltpu.VMEM((4, RADIX, OWN, LANES), F32),
            pltpu.VMEM((4, RADIX, OWN, LANES), F32),
            pltpu.VMEM((COLS, COLS), BF16),
            pltpu.VMEM((COLS, COLS), BF16),
            pltpu.VMEM((3, 2, 2, 1, WIDTH), F32),
            pltpu.VMEM((3, 2, 2, 1, WIDTH), F32),
            pltpu.VMEM((RADIX, OWN, LANES), F32),
            pltpu.VMEM((NGX, 1, COLS), F32),
            pltpu.VMEM((NGX, 1, COLS), F32),
            pltpu.VMEM((1, COLS), F32),
            pltpu.VMEM((4, 1, COLS), F32),
            pltpu.VMEM((1, COLS), F32),
            pltpu.VMEM((8, 1, COLS), F32),
            pltpu.VMEM((6, NGX, OWN, COLS), BF16),
            pltpu.VMEM((NGX, OWN, LANES), F32),
            dma((6,)),
            dma((20, NGX)),
            dma((20, NGX)),
            dma((2,)),
            dma((2,)),
            dma((3, 2)),
            dma((3, 2)),
            dma((4,)),
            dma((4,)),
            dma((8,)),
            dma((8,)),
        ],
        compiler_params=pltpu.CompilerParams(collective_id=0, has_side_effects=True),
        name="exchange",
    )(p, q, c, m, f, bw, n, g, l, jnp.asarray(mats), jnp.asarray(small))

    parts = 4
    per, rows = NGX // parts, ROWS // parts
    pair = pl.BlockSpec((2, rows, COLS), lambda i: (0, i, 0))
    single = pl.BlockSpec((rows, COLS), lambda i: (i, 0))
    line = pl.BlockSpec((1, COLS), lambda i: (0, 0))
    po, qo, co, mo, so = pl.pallas_call(
        functools.partial(final_kernel, edge=None),
        grid=(parts,),
        out_shape=(
            jax.ShapeDtypeStruct(p.shape, F32),
            jax.ShapeDtypeStruct(q.shape, F32),
            jax.ShapeDtypeStruct(c.shape, F32),
            jax.ShapeDtypeStruct(m.shape, F32),
            jax.ShapeDtypeStruct((1, COLS), F32),
        ),
        in_specs=[
            pl.BlockSpec((6, per, OWN, COLS), lambda i: (0, i, 0, 0)),
            pl.BlockSpec((per, OWN, LANES), lambda i: (i, 0, 0)),
            line,
            pl.BlockSpec((1, 2, rows, COLS), lambda i: (0, 0, i, 0)),
            pl.BlockSpec((1, 2, rows, COLS), lambda i: (0, 0, i, 0)),
            pl.BlockSpec((1, rows, COLS), lambda i: (0, i, 0)),
            pl.BlockSpec((1, rows, COLS), lambda i: (0, i, 0)),
            single,
        ],
        out_specs=(pair, pair, single, single, line),
        name="last_step",
    )(codes, edges, sums, f, bw, n, g, l)
    return po, qo, co, mo, so.reshape(COLS)


def solution(mesh):
    in_specs = (
        P(None, "gz", "gx"),
        P(None, "gz", "gx"),
        P("gz", "gx"),
        P("gz", "gx"),
        P(None, None, "gz", "gx"),
        P(None, None, "gz", "gx"),
        P(None, "gz", "gx"),
        P(None, "gz", "gx"),
        P("gz", "gx"),
    )
    out_specs = (
        P(None, "gz", "gx"),
        P(None, "gz", "gx"),
        P("gz", "gx"),
        P("gz", "gx"),
        P("gx"),
    )
    return jax.shard_map(
        per_device, mesh=mesh, in_specs=in_specs, out_specs=out_specs, check_vma=False
    )
```

profile of v0, /device:TPU:1, one launch (start us, length us, event | category | flops | bytes accessed | tf_op | source)
XLA Modules:
  0.0 63.7 jit_solution(1559648478159907719)
XLA Ops:
  0.6 59.7 %exchange.1 = (bf16[6,8,8,256]{3,2,1,0:T(8,128)(2,1)}, f32[8,8,128]{2,1,0:T(8,128)}, f32[1,256]{1,0:T(1,128)}) custom-call(f32[2,64,256]{2,1,0:T(8,128)} %p_h.1, f32[2,64,256]{2,1,0:T(8,128)} %q_h.1, f32[64,256]{1,0:T(8,128)} %c_h.1, f32[64,256]{1,0:T(8,128)} %m_h.1, bf16[4,2,64,256]{3,2,1,0:T(8,128)(2,1)} %f.1, bf16[4,2,64,256]{3,2,1,0:T(8,128)(2,1)} %bw.1, ...), custom_call_target="tpu_custom_call" | custom-call | tf_op jit(solution)/shard_map/exchange/pallas_call | solution.py:507
  60.3 3.3 %last_step.1 = (f32[2,64,256]{2,1,0:T(8,128)}, f32[2,64,256]{2,1,0:T(8,128)}, f32[64,256]{1,0:T(8,128)}, f32[64,256]{1,0:T(8,128)}, f32[1,256]{1,0:T(1,128)}) custom-call(bf16[6,8,8,256]{3,2,1,0:T(8,128)(2,1)} %get-tuple-element.13.oc, f32[8,8,128]{2,1,0:T(8,128)} %get-tuple-element.14.oe, f32[1,256]{1,0:T(1,128)} %get-tuple-element.15.os, ...), custom_call_target="tpu_custom_call" | custom-call | tf_op jit(solution)/shard_map/last_step/pallas_call | solution.py:564
where the time goes:
time: 63.9 us; the launch traced here: 63.7 us
  Pallas kernels  63 us (99%)
  between operations  0.64 us (1%)
    pallas_call x1, Pallas kernels, per_device(): pl.pallas_call(exchange_kernel, out_shape=(jax.ShapeDtypeStruct((6, NGX,...  59.7 us
    pallas_call x1, Pallas kernels, per_device(): pl.pallas_call(functools.partial(final_kernel, edge=None), grid=(parts,),...  3.34 us

commit v1 on v0

--- a/solution.py
+++ b/solution.py
@@ -116,29 +116,34 @@
 
 
 def diffract(uv, out, w, tb, xh, xl):
+    tile = 8 * RADIX
     for field in range(2):
         points = [(uv[2 * field, a], uv[2 * field + 1, a]) for a in range(RADIX)]
         for k, (re, im) in enumerate(dft(points, -1.0)):
             c, s = tb[0, k : k + 1, :], tb[1, k : k + 1, :]
-            row = pl.ds(16 * k + 8 * field, 8)
+            row = pl.ds(tile * field + 8 * k, 8)
             h, l = split(re * c + im * s)
             xh[row, 0:LANES], xl[row, 0:LANES] = h, l
             h, l = split(im * c - re * s)
             xh[row, LANES:], xl[row, LANES:] = h, l
-    spectrum = product(xh, xl, w, 0)
-    for k in range(RADIX):
-        row = slice(16 * k, 16 * k + 16)
-        c, s = tb[2, k : k + 1, :], tb[3, k : k + 1, :]
-        re, im = spectrum[row, :LANES], spectrum[row, LANES:]
-        h, l = split(re * c - im * s)
-        xh[row, 0:LANES], xl[row, 0:LANES] = h, l
-        h, l = split(re * s + im * c)
-        xh[row, LANES:], xl[row, LANES:] = h, l
-    back = product(xh, xl, w, 1)
     for field in range(2):
+        half = pl.ds(tile * field, tile)
+        spectrum = product(xh.at[half], xl.at[half], w, 0)
+        for k in range(RADIX):
+            row = slice(8 * k, 8 * k + 8)
+            c, s = tb[2, k : k + 1, :], tb[3, k : k + 1, :]
+            re, im = spectrum[row, :LANES], spectrum[row, LANES:]
+            at = pl.ds(tile * field + 8 * k, 8)
+            h, l = split(re * c - im * s)
+            xh[at, 0:LANES], xl[at, 0:LANES] = h, l
+            h, l = split(re * s + im * c)
+            xh[at, LANES:], xl[at, LANES:] = h, l
+    for field in range(2):
+        half = pl.ds(tile * field, tile)
+        back = product(xh.at[half], xl.at[half], w, 1)
         points = []
         for k in range(RADIX):
-            row = slice(16 * k + 8 * field, 16 * k + 8 * field + 8)
+            row = slice(8 * k, 8 * k + 8)
             c, s = tb[0, k : k + 1, :], tb[1, k : k + 1, :]
             re, im = back[row, :LANES], back[row, LANES:]
             points.append((re * c - im * s, im * c + re * s))
@@ -202,14 +207,31 @@
 def exchange_kernel(
     p_h, q_h, c_h, m_h, f_h, b_h, n_h, g_h, l_h, w_h, t_h,
     oc, oe, os,
-    pq, w, tb, ch, co, ax, rc, ra, rh, rl, st, uv, vv, xh, xl,
+    pq, w, tb, ch, co, ax, rc, ra, sg, rh, st, uv, vv, xh, xl,
     hs, hr, sacc, sb, sr, s2b, s2, s3b, s3, vo, eo,
-    ls, ss, rs, cs, cr, hss, hrs, ys, yr, zs, zr,
+    ls, ss, rs, cs, cr, hss, hrs, zs, zr,
 ):
     g, b = lax.axis_index("gz"), lax.axis_index("gx")
     me = place_of(g, b)
-    y, r = lax.div(g, 8), lax.rem(g, 8)
     started = []
+
+    g_up, g_down = lax.rem(g + 1, NGZ), lax.rem(g + NGZ - 1, NGZ)
+    chain = g * NGX + me
+    after = lax.rem(chain + 1, NGZ * NGX)
+    before = lax.rem(chain + NGZ * NGX - 1, NGZ * NGX)
+
+    def row_device(q):
+        qg = lax.div(q, NGX)
+        return qg, owner_of(qg, lax.rem(q, NGX))
+
+    dev_after, dev_before = row_device(after), row_device(before)
+    x_peers = [(g, lax.rem(b + k, NGX)) for k in range(1, NGX)]
+    z_peers = [(lax.rem(g + 2 * k, NGZ), b) for k in range(1, NGZ // 2)]
+    twin = (g + 1 - 2 * lax.rem(g, 2), b)
+    greet = x_peers + z_peers + [twin, (g_up, b), (g_down, b), dev_after, dev_before]
+    barrier = pltpu.get_barrier_semaphore()
+    for peer in greet:
+        pl.semaphore_signal(barrier, inc=1, device_id=peer, device_id_type=MESH)
 
     loads = [
         (p_h, pq.at[0:2]),
@@ -218,29 +240,59 @@
         (m_h, pq.at[5]),
         (w_h, w),
         (t_h, tb),
+        (l_h, sg.at[6]),
     ]
-    loads = [pltpu.make_async_copy(a, d, ls.at[i]) for i, (a, d) in enumerate(loads)]
-    for load in loads:
+    for step, base in ((3, 0), (2, 7), (1, 13)):
+        loads += [
+            (f_h.at[step], sg.at[base : base + 2]),
+            (b_h.at[step], sg.at[base + 2 : base + 4]),
+            (n_h.at[step], sg.at[base + 4]),
+            (g_h.at[step], sg.at[base + 5]),
+        ]
+    loads = [pltpu.make_async_copy(src, dst, ls.at[i]) for i, (src, dst) in enumerate(loads)]
+    for load in loads[6:11] + loads[:6] + loads[11:]:
         load.start()
 
-    g_up, g_down = lax.rem(g + 1, NGZ), lax.rem(g + NGZ - 1, NGZ)
-    chain = g * NGX + me
-    after = lax.rem(chain + 1, NGZ * NGX)
-    before = lax.rem(chain + NGZ * NGX - 1, NGZ * NGX)
-
-    def row_device(q):
-        qg = lax.div(q, NGX)
-        return qg, owner_of(qg, lax.rem(q, NGX))
-
-    dev_after, dev_before = row_device(after), row_device(before)
-    y_peers = [(lax.rem(y + k, 4) * 8 + r, b) for k in range(1, 4)]
-    z_peers = [(y * 8 + lax.rem(r + k, 8), b) for k in range(1, 8)]
-    x_peers = [(g, lax.rem(b + k, NGX)) for k in range(1, NGX)]
-    greet = x_peers + y_peers + z_peers + [(g_up, b), (g_down, b), dev_after, dev_before]
-    barrier = pltpu.get_barrier_semaphore()
-    for peer in greet:
-        pl.semaphore_signal(barrier, inc=1, device_id=peer, device_id_type=MESH)
-
+    pl.semaphore_wait(barrier, len(greet))
+
+    def remote(src, dst, send, recv, device):
+        copy = pltpu.make_async_remote_copy(
+            src_ref=src, dst_ref=dst, send_sem=send, recv_sem=recv,
+            device_id=device, device_id_type=MESH,
+        )
+        copy.start()
+        started.append(copy)
+        return copy
+
+    edge = [
+        remote(p_h.at[:, 0:8, :], ch.at[0], cs.at[0], cr.at[0], (g_down, b)),
+        remote(q_h.at[:, 56:64, :], ch.at[1], cs.at[1], cr.at[1], (g_up, b)),
+    ]
+
+    def spread(ident, src_of, dst):
+        got = []
+        for k in range(1, NGX):
+            peer = lax.rem(b + k, NGX)
+            src = src_of(peer, place_of(g, peer))
+            got.append(remote(src, dst, ss.at[ident, k], rs.at[ident, k], (g, peer)))
+        own = pltpu.make_async_copy(src_of(b, me), dst, rs.at[ident, 0])
+        own.start()
+        return got, own
+
+    def arrive(group):
+        for copies, own in group:
+            for copy in copies:
+                copy.wait_recv()
+            own.wait()
+
+    def planes(ident, first, last):
+        return [
+            spread(ident, lambda _, j: sg.at[first:last, rows_at(j), :], rh.at[first:last, b])
+        ]
+
+    for load in loads[6:11]:
+        load.wait()
+    got_hist = {3: planes(3, 0, 7)}
     for load in loads[:4]:
         load.wait()
     top_c = largest(jnp.max(jnp.abs(pq[4]).reshape(8, 8, COLS), axis=0))
@@ -254,50 +306,6 @@
             rows = slice(8 * t, 8 * t + 8)
             co[i, rows] = encode(pq[i, rows], inv).astype(BF16)
 
-    pl.semaphore_wait(barrier, len(greet))
-
-    def remote(src, dst, send, recv, device):
-        copy = pltpu.make_async_remote_copy(
-            src_ref=src, dst_ref=dst, send_sem=send, recv_sem=recv,
-            device_id=device, device_id_type=MESH,
-        )
-        copy.start()
-        started.append(copy)
-        return copy
-
-    edge = [
-        remote(p_h.at[:, 0:8, :], ch.at[0], cs.at[0], cr.at[0], (g_down, b)),
-        remote(q_h.at[:, 56:64, :], ch.at[1], cs.at[1], cr.at[1], (g_up, b)),
-    ]
-
-    def spread(ident, src_of, dst):
-        got = []
-        for k in range(1, NGX):
-            peer = lax.rem(b + k, NGX)
-            src = src_of(peer, place_of(g, peer))
-            got.append(remote(src, dst, ss.at[ident, k], rs.at[ident, k], (g, peer)))
-        own = pltpu.make_async_copy(src_of(b, me), dst, rs.at[ident, 0])
-        own.start()
-        return got, own
-
-    def arrive(group):
-        for copies, own in group:
-            for copy in copies:
-                copy.wait_recv()
-            own.wait()
-
-    def history(step):
-        base = 3 + 4 * (3 - step) + (1 if step < 3 else 0)
-        slot = rh.at[3 - step]
-        return [
-            spread(base, lambda _, j: f_h.at[step, :, rows_at(j), :], slot.at[0:2, b]),
-            spread(base + 1, lambda _, j: b_h.at[step, :, rows_at(j), :], slot.at[2:4, b]),
-            spread(base + 2, lambda _, j: n_h.at[step, rows_at(j), :], slot.at[4, b]),
-            spread(base + 3, lambda _, j: g_h.at[step, rows_at(j), :], slot.at[5, b]),
-        ]
-
-    got_hist = {3: history(3)}
-    got_loss = [spread(7, lambda _, j: l_h.at[rows_at(j), :], rl.at[b])]
     got_cm = [spread(0, lambda _, j: co.at[4:6, rows_at(j), :], rc.at[4:6, b])]
 
     for copy in edge:
@@ -332,9 +340,14 @@
     ax[...] = jnp.where(row == 0, sc_u, jnp.where(row == 1, sc_c, sc_m))
     got_ax = [spread(2, lambda _, j: ax, ra.at[b])]
     got_uv = [spread(1, lambda _, j: co.at[0:4, rows_at(j), :], rc.at[0:4, b])]
-    got_hist[2] = history(2)
-
-    for load in loads[4:]:
+    for load in loads[11:15]:
+        load.wait()
+    got_hist[2] = planes(4, 7, 13)
+    for load in loads[15:]:
+        load.wait()
+    got_hist[1] = planes(5, 13, 17) + planes(6, 17, 19)
+
+    for load in loads[4:6]:
         load.wait()
     arrive(got_ax)
     arrive(got_uv)
@@ -343,11 +356,9 @@
         scale = ra[src, 0:1, :]
         for i in range(4):
             uv[i, a] = decode(rc[i, src, :, half], scale)
-    got_hist[1] = history(1)
     diffract(uv, vv, w, tb, xh, xl)
 
     arrive(got_cm)
-    arrive(got_loss)
     for a in range(RADIX):
         src, half = a // 2, pl.ds(LANES * (a % 2), LANES)
         for i in (4, 5):
@@ -372,6 +383,7 @@
     halos = None
     for step in (3, 2, 1):
         slot = 3 - step
+        base = (0, 7, 13)[slot]
         arrive(got_hist[step])
         laps = []
         for a in range(RADIX):
@@ -379,10 +391,10 @@
             uv[0, a] = right - 2.0 * c + left
         for a in range(RADIX):
             src, half = a // 2, pl.ds(LANES * (a % 2), LANES)
-            past = [rh[slot, i, src, :, half].astype(F32) for i in range(6)]
+            past = [rh[base + i, src, :, half].astype(F32) for i in range(6)]
             new = revised(
                 [vv[i, a] for i in range(4)], past[:4], past[4], past[5],
-                rl[src, :, half].astype(F32), st[4, a], st[5, a], uv[0, a],
+                rh[6, src, :, half].astype(F32), st[4, a], st[5, a], uv[0, a],
             )
             for i in range(6):
                 st[i, a] = new[i]
@@ -398,7 +410,7 @@
             for a in range(RADIX):
                 half = pl.ds(LANES * (a % 2), LANES)
                 sb[a // 2, :, half] = jnp.sum(sacc[a], axis=0, keepdims=True)
-            got_s = [spread(19, lambda peer, j: sb.at[peer], sr.at[b])]
+            got_s = [spread(10, lambda peer, j: sb.at[peer], sr.at[b])]
             scales = []
             for i in (4, 5):
                 top = jnp.abs(st[i, 0])
@@ -410,9 +422,17 @@
                 for a in range(RADIX):
                     half = pl.ds(LANES * (a % 2), LANES)
                     vo[i, a // 2, :, half] = encode(st[i, a], inv).astype(BF16)
-            got_out = [spread(16, lambda peer, j: vo.at[4:6, peer], oc.at[4:6, me])]
+            got_out = [spread(7, lambda peer, j: vo.at[4:6, peer], oc.at[4:6, me])]
         for copy in halos:
             copy.wait_recv()
+        if step == 1:
+            arrive(got_s)
+            total = sr[0]
+            for k in range(1, NGX):
+                total = total + sr[k]
+            s3b[...] = total
+            s3[lax.rem(g, 2)] = total
+            pair = remote(s3b, s3.at[lax.rem(g, 2)], zs.at[0], zr.at[0], twin)
         energy = [jnp.zeros((OWN, LANES), F32), jnp.zeros((OWN, LANES), F32)]
         for a in range(RADIX):
             cols = pl.ds(LANES * a, LANES)
@@ -439,38 +459,28 @@
                 _, _, right = lateral(2 * block + 1)
                 tile = jnp.where(lane == 0, left, marks)
                 eo[block] = jnp.where(lane == LANES - 1, right, tile)
-            got_out.append(spread(17, lambda peer, j: eo.at[peer], oe.at[me]))
-            arrive(got_s)
-            total = sr[0]
-            for k in range(1, NGX):
-                total = total + sr[k]
+            got_out.append(spread(8, lambda peer, j: eo.at[peer], oe.at[me]))
+            pair.wait_recv()
+            total = s3[0] + s3[1]
             s2b[...] = total
-            s2[0] = total
-            got_y = [
-                remote(s2b, s2.at[k], ys.at[k], yr.at[k], peer)
-                for k, peer in enumerate(y_peers, 1)
+            s2[lax.div(g, 2)] = total
+            got_z = [
+                remote(s2b, s2.at[lax.div(g, 2)], zs.at[k], zr.at[k], peer)
+                for k, peer in enumerate(z_peers, 1)
             ]
         diffract(uv, vv, w, tb, xh, xl)
 
-    for copy in got_y:
-        copy.wait_recv()
-    total = (s2[0] + s2[1]) + (s2[2] + s2[3])
-    s3b[...] = total
-    s3[0] = total
-    got_z = [
-        remote(s3b, s3.at[k], zs.at[k], zr.at[k], peer) for k, peer in enumerate(z_peers, 1)
-    ]
     inv = 1.0 / sc_v
     for a in range(RADIX):
         half = pl.ds(LANES * (a % 2), LANES)
         for i in range(4):
             vo[i, a // 2, :, half] = encode(vv[i, a], inv).astype(BF16)
-    got_out.append(spread(18, lambda peer, j: vo.at[0:4, peer], oc.at[0:4, me]))
+    got_out.append(spread(9, lambda peer, j: vo.at[0:4, peer], oc.at[0:4, me]))
     for copy in got_z:
         copy.wait_recv()
-    total = s3[0]
-    for k in range(1, NGX):
-        total = total + s3[k]
+    total = s2[0]
+    for k in range(1, NGZ // 2):
+        total = total + s2[k]
     os[...] = total * (CLOCK_DELTA / math.sqrt(ROWS * NGZ))
     arrive(got_out)
     for copy in started:
@@ -522,8 +532,8 @@
             pltpu.VMEM((OWN, LANES), F32),
             pltpu.VMEM((6, NGX, OWN, COLS), BF16),
             pltpu.VMEM((NGX, OWN, LANES), F32),
-            pltpu.VMEM((3, 6, NGX, OWN, COLS), BF16),
-            pltpu.VMEM((NGX, OWN, COLS), BF16),
+            pltpu.VMEM((19, ROWS, COLS), BF16),
+            pltpu.VMEM((19, NGX, OWN, COLS), BF16),
             pltpu.VMEM((6, RADIX, OWN, LANES), F32),
             pltpu.VMEM((4, RADIX, OWN, LANES), F32),
             pltpu.VMEM((4, RADIX, OWN, LANES), F32),
@@ -535,28 +545,26 @@
             pltpu.VMEM((NGX, 1, COLS), F32),
             pltpu.VMEM((NGX, 1, COLS), F32),
             pltpu.VMEM((1, COLS), F32),
-            pltpu.VMEM((4, 1, COLS), F32),
+            pltpu.VMEM((NGZ // 2, 1, COLS), F32),
             pltpu.VMEM((1, COLS), F32),
-            pltpu.VMEM((8, 1, COLS), F32),
+            pltpu.VMEM((2, 1, COLS), F32),
             pltpu.VMEM((6, NGX, OWN, COLS), BF16),
             pltpu.VMEM((NGX, OWN, LANES), F32),
-            dma((6,)),
-            dma((20, NGX)),
-            dma((20, NGX)),
+            dma((19,)),
+            dma((11, NGX)),
+            dma((11, NGX)),
             dma((2,)),
             dma((2,)),
             dma((3, 2)),
             dma((3, 2)),
-            dma((4,)),
-            dma((4,)),
-            dma((8,)),
-            dma((8,)),
+            dma((NGZ // 2,)),
+            dma((NGZ // 2,)),
         ],
         compiler_params=pltpu.CompilerParams(collective_id=0, has_side_effects=True),
         name="exchange",
     )(p, q, c, m, f, bw, n, g, l, jnp.asarray(mats), jnp.asarray(small))
 
-    parts = 4
+    parts = 2
     per, rows = NGX // parts, ROWS // parts
     pair = pl.BlockSpec((2, rows, COLS), lambda i: (0, i, 0))
     single = pl.BlockSpec((rows, COLS), lambda i: (i, 0))

time: 63.9 us -> 60.7 us (0.950)
  Pallas kernels: 63 us -> 60 us
    pallas_call x1, Pallas kernels: 59.7 us -> 57.8 us  [per_device(): pl.pallas_call(exchange_kernel, out_shape=(jax.ShapeDtypeStruct((6, NGX,...]
    pallas_call x1, Pallas kernels: 3.34 us -> 2.15 us  [per_device(): pl.pallas_call(functools.partial(final_kernel, edge=None), grid=(parts,),...]
where the time goes in v1:
time: 60.7 us; the launch traced here: 60.6 us
  Pallas kernels  60 us (99%)
  between operations  0.64 us (1%)
    pallas_call x1, Pallas kernels, per_device(): pl.pallas_call(exchange_kernel, out_shape=(jax.ShapeDtypeStruct((6, NGX,...  57.8 us
    pallas_call x1, Pallas kernels, per_device(): pl.pallas_call(functools.partial(final_kernel, edge=None), grid=(parts,),...  2.15 us

profile of v1, /device:TPU:1, one launch (start us, length us, event | category | flops | bytes accessed | tf_op | source)
XLA Modules:
  0.0 60.6 jit_solution(7700967254894029066)
XLA Ops:
  0.6 57.8 %exchange.1 = (bf16[6,8,8,256]{3,2,1,0:T(8,128)(2,1)}, f32[8,8,128]{2,1,0:T(8,128)}, f32[1,256]{1,0:T(1,128)}) custom-call(f32[2,64,256]{2,1,0:T(8,128)} %p_h.1, f32[2,64,256]{2,1,0:T(8,128)} %q_h.1, f32[64,256]{1,0:T(8,128)} %c_h.1, f32[64,256]{1,0:T(8,128)} %m_h.1, bf16[4,2,64,256]{3,2,1,0:T(8,128)(2,1)} %f.1, bf16[4,2,64,256]{3,2,1,0:T(8,128)(2,1)} %bw.1, ...), custom_call_target="tpu_custom_call" | custom-call | tf_op jit(solution)/shard_map/exchange/pallas_call | solution.py:517
  58.4 2.2 %last_step.1 = (f32[2,64,256]{2,1,0:T(8,128)}, f32[2,64,256]{2,1,0:T(8,128)}, f32[64,256]{1,0:T(8,128)}, f32[64,256]{1,0:T(8,128)}, f32[1,256]{1,0:T(1,128)}) custom-call(bf16[6,8,8,256]{3,2,1,0:T(8,128)(2,1)} %get-tuple-element.13.oc, f32[8,8,128]{2,1,0:T(8,128)} %get-tuple-element.14.oe, f32[1,256]{1,0:T(1,128)} %get-tuple-element.15.os, ...), custom_call_target="tpu_custom_call" | custom-call | tf_op jit(solution)/shard_map/last_step/pallas_call | solution.py:572
